TPU v7x, 256 devices: a whole 4x4x8 slice. The times are simulated.
256 devices in a mesh: row: 16 (over z, core), col: 16 (over x, y).
Axes of the slice: x: 4, y: 4, z: 8, core: 2. Of those that a mesh axis runs over, the one named last changes fastest.
Arguments:
- factor: float32 [1, 16, 896, 1, 16, 896], P(None, 'row', None, None, 'col'), as said below
- damping: float32 [1], replicated, may hold values from 0.1 to 1
Outputs:
- factor_state: float32 [1, 16, 896, 1, 16, 896], P(None, 'row', None, None, 'col')
Inputs may be any that keep to these rules, and one draw needn't show every extreme that they name: factor is symmetric and positive semidefinite, so that A's smallest eigenvalue is at least damping[0].
All inputs are finite; a program needn't handle non-finite values.
Results may differ from a plain program's by a relative error of at most 0.00016.
Values sent between devices are 32-bit elements; how exact they have to be, the bound alone decides.
No kernel may reach another device: no remote copies, remote signals or barrier semaphores. Data moves between devices by JAX's collectives and lax.ppermute only.
A program may use at most 128 MiB of HBM per device.

v0:
```python
import jax
import jax.numpy as jnp
from jax import lax
from jax.sharding import PartitionSpec as P


def broadcast(array, axis, root):
    mine = lax.axis_index(axis) == root
    return lax.psum(jnp.where(mine, array, jnp.zeros_like(array)), axis)


def times_transposed(left, right):
    return lax.dot_general(
        left,
        right,
        (((1,), (1,)), ((), ())),
        precision=lax.Precision.HIGHEST,
        preferred_element_type=jnp.float32,
    )


def on_device(factor, damping):
    grid_rows = lax.axis_size("row")
    grid_cols = lax.axis_size("col")
    row_index = lax.axis_index("row")
    col_index = lax.axis_index("col")
    tile_rows = factor.shape[0]
    tile_cols = factor.shape[3]
    tile_order = factor.shape[2]
    strip_rows = tile_order // grid_cols
    first_axis = lax.broadcasted_iota(jnp.int32, (tile_order, tile_order), 0)
    second_axis = lax.broadcasted_iota(jnp.int32, (tile_order, tile_order), 1)
    identity = (first_axis == second_axis).astype(jnp.float32)
    empty = jnp.zeros((tile_order, tile_order), jnp.float32)
    row_ids = [0 + row_index]
    col_ids = [0 + col_index]
    tiles = [
        [factor[0, 0, :, 0, 0, :] + jnp.where(row_ids[0] == col_ids[0], damping[0], 0.0) * identity]
    ]

    def factor_tile(square):
        lower = jnp.linalg.cholesky(square)
        return (lower, jax.scipy.linalg.solve_triangular(lower, identity, lower=True))

    def skip_factor(square):
        return (empty, empty)

    def solve_all(blocks, inverse):
        return jnp.stack([times_transposed(blocks[0], inverse)])

    def solve_none(blocks, inverse):
        return jnp.zeros_like(blocks)

    panels = []

    def apply_panel(square, row_slot, col_slot, panel_id):
        return square - times_transposed(
            panels[panel_id][0][row_slot], panels[panel_id][1][col_slot]
        )

    home_row = 0 % grid_rows
    home_col = 0 % grid_cols
    slot_row = 0 // grid_rows
    slot_col = 0 // grid_cols
    is_home = jnp.logical_and(row_index == home_row, col_index == home_col)
    in_panel = col_index == home_col
    diag_lower, diag_inverse = lax.cond(
        is_home, factor_tile, skip_factor, tiles[slot_row][slot_col]
    )
    own_blocks = jnp.stack([tiles[0][slot_col]])
    inverse_here = broadcast(diag_inverse, "row", home_row)
    solved_own = lax.cond(in_panel, solve_all, solve_none, own_blocks, inverse_here)
    outgoing = jnp.stack(
        [jnp.where(row_ids[0] > 0, solved_own[0], jnp.where(row_ids[0] == 0, diag_lower, 0.0))]
    )
    strips = lax.all_to_all(outgoing, "col", split_axis=1, concat_axis=1, tiled=True)
    home_strip = lax.slice_in_dim(
        strips, home_col * strip_rows, (home_col + 1) * strip_rows, axis=1
    )
    arrived = lax.all_gather(home_strip, "col", axis=1, tiled=True)
    row_slot = 0
    tiles[row_slot][slot_col] = jnp.where(in_panel, arrived[row_slot], tiles[row_slot][slot_col])
    col_slot = 0
    wanted = col_ids[col_slot]
    source_slot = wanted // grid_rows
    piece_here = lax.dynamic_index_in_dim(arrived, source_slot, 0, keepdims=False)
    col_pieces = [broadcast(piece_here, "row", wanted % grid_rows)]
    panels.append((arrived, col_pieces))
    row_slot = 0
    col_slot = 0
    chosen = jnp.logical_and(row_ids[row_slot] >= col_ids[col_slot], col_ids[col_slot] > 0)
    tiles[row_slot][col_slot] = lax.cond(
        chosen,
        lambda square, rs=row_slot, cs=col_slot, pid=0: apply_panel(square, rs, cs, pid),
        lambda square: square,
        tiles[row_slot][col_slot],
    )
    row_slot = 0
    kept = [jnp.where(row_ids[row_slot] >= col_ids[0], tiles[row_slot][0], 0.0)]
    finished = [jnp.stack(kept, axis=1)]
    stacked = jnp.stack(finished, axis=0)
    return stacked.reshape(tile_rows, 1, tile_order, tile_cols, 1, tile_order)


def solution(mesh):
    return jax.shard_map(
        on_device,
        mesh=mesh,
        in_specs=(P(None, "row", None, None, "col", None), P()),
        out_specs=P(None, "row", None, None, "col", None),
        check_vma=False,
    )
```

profile of v0, /device:TPU:9, one launch (start us, length us, event | category | flops | bytes accessed | tf_op | source)
XLA Modules:
  0.0 705.8 jit_solution(6807811891235126774)
XLA Ops:
  6.5 0.0 all-reduce.4.cloned.1.call-start
  6.5 1.9 fusion.69
  9.1 2.1 bitcast_add_fusion.1
  11.2 10.6 %conditional.3 = (f32[896,896]{1,0:T(8,128)}, f32[896,896]{1,0:T(8,128)}) conditional(s32[]{:T(128)} %convert_element_type.26, () %tuple.28, (f32[896,896]{1,0:T(8,128)S(1)}, f32[896,896]{1,0:T(8,128)}, f32[896,896]{1,0:T(8,128)}, f32[896,896]{1,0:T(8,128)}, f32[896,896]{1,0:T(8,128)}, /*index=5*/f32[896,896]{1,0:T(8,128)}, f32[896,896]{1,0:T(8,128)}, ...), branch_computations={%region_0.1_spmd, %region_1.16_spmd} | conditional | flops 6878954496 | bytes 101458848 | solution.py:67
  11.2 1.9 broadcast.318
  13.2 1.9 broadcast.318.clone
  21.9 1.9 broadcast_select_fusion
  23.8 0.0 all-reduce.4.cloned.1.call-update
  23.8 0.0 all-gather.2.cloned.1.call-start
  23.9 416.9 %all-reduce.4.cloned.1.call-done = f32[896,896]{1,0:T(8,128)} async-done(((f32[896,896]{1,0:T(8,128)}), f32[896,896]{1,0:T(8,128)}) %all-reduce.4.cloned.1.call-update) | async-done | bytes 3211280 | tf_op jit(solution)/shard_map/psum | solution.py:9
  440.8 1.9 conditional.4
  440.8 1.9 squeeze.14
  442.7 2.2 select_select_fusion.1
  444.9 4.7 stack.4
  449.7 53.7 %all_to_all.5 = f32[1,896,896]{2,0,1:T(1,128)S(1)} all-to-all(f32[1,896,896]{2,0,1:T(1,128)S(1)} %stack.4), channel_id=1, replica_groups=mesh['row'=16,'col'=16] {'col'}, dimensions={1} | all-to-all | bytes 6422528 | tf_op jit(solution)/shard_map/all_to_all | solution.py:76
  503.4 0.1 slice.228
  503.4 0.7 copy.10
  504.1 0.0 all-gather.2.cloned.1.call-update
  504.2 0.0 all-reduce.6.cloned.1.call-start
  504.2 49.1 %all-gather.2.cloned.1.call-done = f32[1,896,896]{2,1,0:T(8,128)} async-done(((f32[1,56,896]{2,1,0:T(8,128)}), f32[1,896,896]{2,1,0:T(8,128)}) %all-gather.2.cloned.1.call-update) | async-done | bytes 3211280 | tf_op jit(solution)/shard_map/all_gather | solution.py:80
  553.3 5.3 bitcast_select_fusion
  558.6 0.0 all-reduce.6.cloned.1.call-update
  558.6 119.2 %all-reduce.6.cloned.1.call-done = f32[896,896]{1,0:T(8,128)} async-done(((f32[896,896]{1,0:T(8,128)}), f32[896,896]{1,0:T(8,128)}) %all-reduce.6.cloned.1.call-update) | async-done | bytes 3211280 | tf_op jit(solution)/shard_map/psum | solution.py:9
  677.8 16.0 %conditional.5 = (f32[896,896]{1,0:T(8,128)S(1)}) conditional(s32[]{:T(128)} %convert_element_type.24, f32[896,896]{1,0:T(8,128)S(1)} %get-tuple-element.131, (f32[1,896,896]{2,1,0:T(8,128)}, f32[896,896]{1,0:T(8,128)}, f32[896,896]{1,0:T(8,128)S(1)}) %tuple.31), branch_computations={%region_20.21_spmd, %region_21.22_spmd} | conditional | flops 8632680448 | bytes 12845064 | solution.py:92
  678.2 15.5 %fusion.2 = f32[896,896]{1,0:T(8,128)S(1)} fusion(f32[896,896]{1,0:T(8,128)S(1)} %get-tuple-element.43, f32[896,896]{1,0:T(8,128)} %get-tuple-element.45, f32[1,896,896]{2,1,0:T(8,128)} %get-tuple-element.44), kind=kOutput, calls=%fused_computation.2 | convolution fusion | flops 8632680448 | bytes 12845056 | tf_op jit(solution)/shard_map/cond/branch_1_fun/dot_general | solution.py:13
  693.9 0.2 select_bitcast_fusion.6
  694.1 5.0 copy.8
Async XLA Ops:
  6.5 434.2 %all-reduce.4.cloned.1.call-start = ((), (), s32[]{:S(2)}) async-start(), calls=%async_computation.1 | async-start | bytes 6422528 | tf_op jit(solution)/shard_map/psum | solution.py:9
  23.8 529.5 %all-gather.2.cloned.1.call-start = ((), (), s32[]{:S(2)}) async-start(), calls=%async_computation.2 | async-start | bytes 3411968 | tf_op jit(solution)/shard_map/all_gather | solution.py:80
  504.2 173.7 %all-reduce.6.cloned.1.call-start = ((), (), s32[]{:S(2)}) async-start(), calls=%async_computation.3 | async-start | bytes 6422528 | tf_op jit(solution)/shard_map/psum | solution.py:9
Sparse Core Ops, SparseCore 0:
  23.9 416.7 all-reduce.3
  504.3 48.9 all-gather.1
  558.7 119.0 all-reduce.5
where the time goes:
time: 717 us; the launch traced here: 706 us
  waiting for transfers between devices  585 us (82%)
  blocking collectives  53.7 us (7%)
  local copies, waits for them, and re-layouts  16.2 us (2%)
  matrix products  15.5 us (2%)
  between operations  14 us (2%)
  other arithmetic  13.7 us (2%)
  loops' own time  7.36 us (1%)
    psum x2, waiting for transfers between devices, broadcast(): return lax.psum(jnp.where(mine, array, jnp.zeros_like(array)), axis)  536 us
    all_to_all x1, blocking collectives, on_device(): lax.all_to_all(outgoing, 'col', split_axis=1, concat_axis=1, tiled=True)  53.7 us
    all_gather x1, waiting for transfers between devices, on_device(): arrived = lax.all_gather(home_strip, 'col', axis=1, tiled=True)  49.1 us
    dot_general x1, matrix products, times_transposed(): lax.dot_general(left, right, (((1,), (1,)), ((), ())), precision=lax.Prec...  15.5 us
  transfers between devices with their start and end apart: 3, of which 3 were waited for; matrix products, arithmetic and copies ran while one was open for 0% of the time, Pallas kernels for 0%

commit v1 on v0

--- a/solution.py
+++ b/solution.py
@@ -4,9 +4,15 @@
 from jax.sharding import PartitionSpec as P
 
 
+def add_all(x, name):
+    parts = lax.all_gather(x, name, axis=0, tiled=False)
+    result = parts.sum(axis=0)
+    return result
+
+
 def broadcast(array, axis, root):
     mine = lax.axis_index(axis) == root
-    return lax.psum(jnp.where(mine, array, jnp.zeros_like(array)), axis)
+    return add_all(jnp.where(mine, array, jnp.zeros_like(array)), axis)
 
 
 def times_transposed(left, right):

time: 717 us -> 1030 us (1.44)
  waiting for transfers between devices: 585 us -> 857 us
  other arithmetic: 13.7 us -> 57 us
    all_gather x0 -> x2, waiting for transfers between devices: none -> 809 us  [add_all(): parts = lax.all_gather(x, name, axis=0, tiled=False)]
    psum x2 -> x0, waiting for transfers between devices: 536 us -> none  [broadcast(): return lax.psum(jnp.where(mine, array, jnp.zeros_like(array)), axis)]
    reduce_sum x0 -> x2, other arithmetic: none -> 39 us  [add_all(): result = parts.sum(axis=0)]
where the time goes in v1:
time: 1030 us; the launch traced here: 1020 us
  waiting for transfers between devices  857 us (83%)
  other arithmetic  57 us (6%)
  blocking collectives  54 us (5%)
  local copies, waits for them, and re-layouts  18.1 us (2%)
  matrix products  14.9 us (1%)
  between operations  14.1 us (1%)
    all_gather x2, waiting for transfers between devices, add_all(): parts = lax.all_gather(x, name, axis=0, tiled=False)  809 us
    all_to_all x1, blocking collectives, on_device(): lax.all_to_all(outgoing, 'col', split_axis=1, concat_axis=1, tiled=True)  54 us
    all_gather x1, waiting for transfers between devices, on_device(): arrived = lax.all_gather(home_strip, 'col', axis=1, tiled=True)  48.3 us
    reduce_sum x2, other arithmetic, add_all(): result = parts.sum(axis=0)  39 us
  transfers between devices with their start and end apart: 3, of which 3 were waited for; matrix products, arithmetic and copies ran while one was open for 0% of the time, Pallas kernels for 0%

profile of v1, /device:TPU:9, one launch (start us, length us, event | category | flops | bytes accessed | tf_op | source)
XLA Modules:
  0.0 1022.9 jit_solution(8562571703228158040)
XLA Ops:
  6.5 0.0 all-gather.9.cloned.1.call-start
  6.5 1.9 fusion.69
  9.1 2.1 bitcast_add_fusion.1
  11.2 11.3 %conditional.3 = (f32[896,896]{1,0:T(8,128)}, f32[896,896]{1,0:T(8,128)}) conditional(s32[]{:T(128)} %convert_element_type.26, () %tuple.28, (f32[896,896]{1,0:T(8,128)S(1)}, f32[896,896]{1,0:T(8,128)}, f32[896,896]{1,0:T(8,128)}, f32[896,896]{1,0:T(8,128)}, f32[896,896]{1,0:T(8,128)}, /*index=5*/f32[896,896]{1,0:T(8,128)}, f32[896,896]{1,0:T(8,128)}, ...), branch_computations={%region_0.1_spmd, %region_1.16_spmd} | conditional | flops 6878954496 | bytes 101458848 | solution.py:73
  11.2 1.9 broadcast.321
  13.2 1.9 broadcast.321.clone
  22.6 1.9 broadcast_select_fusion.1
  24.5 0.0 all-gather.9.cloned.1.call-update
  24.5 0.0 all-gather.5.cloned.1.call-start
  24.5 556.3 %all-gather.9.cloned.1.call-done = f32[14336,896]{1,0:T(8,128)} async-done(((f32[896,896]{1,0:T(8,128)}), f32[14336,896]{1,0:T(8,128)}) %all-gather.9.cloned.1.call-update) | async-done | bytes 51380240 | tf_op jit(solution)/shard_map/all_gather | solution.py:8
  580.8 19.5 %reduce_sum.18 = f32[896,896]{1,0:T(8,128)} reduce(f32[16,896,896]{2,1,0:T(8,128)} %bitcast.108, f32[]{:T(128)} %constant.283.clone.1), dimensions={0}, to_apply=%region_16.17 | reduce | flops 12042240 | bytes 54591492 | tf_op jit(solution)/shard_map/reduce_sum | solution.py:9
  600.3 1.9 conditional.4
  600.3 1.9 squeeze.14
  602.1 2.2 select_select_fusion.1
  604.4 4.7 stack.4
  609.1 54.0 %all_to_all.5 = f32[1,896,896]{2,0,1:T(1,128)S(1)} all-to-all(f32[1,896,896]{2,0,1:T(1,128)S(1)} %stack.4), channel_id=1, replica_groups=mesh['row'=16,'col'=16] {'col'}, dimensions={1} | all-to-all | bytes 6422528 | tf_op jit(solution)/shard_map/all_to_all | solution.py:82
  663.1 0.1 slice.228
  663.1 0.7 copy.10
  663.8 0.0 all-gather.5.cloned.1.call-update
  663.9 0.0 all-gather.7.cloned.1.call-start
  663.9 48.3 %all-gather.5.cloned.1.call-done = f32[1,896,896]{2,1,0:T(8,128)} async-done(((f32[1,56,896]{2,1,0:T(8,128)}), f32[1,896,896]{2,1,0:T(8,128)}) %all-gather.5.cloned.1.call-update) | async-done | bytes 3211280 | tf_op jit(solution)/shard_map/all_gather | solution.py:86
  712.2 3.8 broadcast_select_fusion
  716.0 0.0 copy-start
  716.0 0.0 all-gather.7.cloned.1.call-update
  716.0 1.9 copy-done
  717.9 3.9 bitcast_select_fusion
  721.8 252.8 %all-gather.7.cloned.1.call-done = f32[16,896,896]{2,1,0:T(8,128)} async-done(((f32[1,896,896]{2,1,0:T(8,128)}), f32[16,896,896]{2,1,0:T(8,128)}) %all-gather.7.cloned.1.call-update) | async-done | bytes 51380240 | tf_op jit(solution)/shard_map/all_gather | solution.py:8
  974.6 19.5 %reduce_sum.19 = f32[896,896]{1,0:T(8,128)} reduce(f32[16,896,896]{2,1,0:T(8,128)} %all-gather.7.cloned.1.call-done, f32[]{:T(128)} %constant.283.clone.1), dimensions={0}, to_apply=%region_19.20 | reduce | flops 12042240 | bytes 54591492 | tf_op jit(solution)/shard_map/reduce_sum | solution.py:9
  994.1 14.9 %conditional.5 = (f32[896,896]{1,0:T(8,128)}) conditional(s32[]{:T(128)} %convert_element_type.24, f32[896,896]{1,0:T(8,128)} %bitcast_select_fusion, (f32[1,896,896]{2,1,0:T(8,128)S(1)}, f32[896,896]{1,0:T(8,128)}, f32[896,896]{1,0:T(8,128)}) %tuple.93), branch_computations={%region_20.21_spmd, %region_21.22_spmd} | conditional | flops 8632680448 | bytes 12845064 | solution.py:98
  994.1 14.9 %fusion.2 = f32[896,896]{1,0:T(8,128)} fusion(f32[896,896]{1,0:T(8,128)} %get-tuple-element.43, f32[896,896]{1,0:T(8,128)} %get-tuple-element.45, f32[1,896,896]{2,1,0:T(8,128)S(1)} %get-tuple-element.44), kind=kOutput, calls=%fused_computation.2 | convolution fusion | flops 8632680448 | bytes 12845056 | tf_op jit(solution)/shard_map/cond/branch_1_fun/dot_general | solution.py:19
  1009.1 2.1 select_bitcast_fusion.6
  1011.2 5.0 copy.8
Async XLA Ops:
  6.5 574.3 %all-gather.9.cloned.1.call-start = ((), (), s32[]{:S(2)}) async-start(), calls=%async_computation.3 | async-start | bytes 54591488 | tf_op jit(solution)/shard_map/all_gather | solution.py:8
  24.5 687.7 %all-gather.5.cloned.1.call-start = ((), (), s32[]{:S(2)}) async-start(), calls=%async_computation.1 | async-start | bytes 3411968 | tf_op jit(solution)/shard_map/all_gather | solution.py:86
  663.9 310.8 %all-gather.7.cloned.1.call-start = ((), (), s32[]{:S(2)}) async-start(), calls=%async_computation.2 | async-start | bytes 54591488 | tf_op jit(solution)/shard_map/all_gather | solution.py:8
  716.0 1.9 copy-start
Sparse Core Ops, SparseCore 0:
  24.6 556.1 all-gather.8
  664.0 48.1 all-gather.4
  716.1 258.4 all-gather.6
